TPU v7x, 512 devices: a whole 4x8x8 slice. The times are simulated.
512 devices in a mesh: req: 64 (over x, z, core), wt: 8 (over y).
Axes of the slice: x: 4, y: 8, z: 8, core: 2. Of those that a mesh axis runs over, the one named last changes fastest.
Arguments:
- streams: bfloat16 [4, 32768, 2048], P(None, 'req', 'wt'), may hold values from -6 to 6
- doc_ids: int32 [64, 512], P('req'), may hold values from 0 to 3, never falling along the last dimension, each value on 1 to 256 neighbouring positions
- doc_adapter: int32 [64, 4, 1], P('req'), may hold values from 0 to 15
- width_weights: float32 [4], replicated, may hold values from 0.2 to 1
- stream_mixing: float32 [4, 4], replicated, may hold values from -3 to 3
- depth_static: float32 [4], replicated, may hold values from 0.2 to 1
- depth_dir: bfloat16 [2048, 4], replicated, may hold values from -0.125 to 0.125
- qkv_weight: bfloat16 [2048, 3, 2048], P('req', None, 'wt')
- adapter_down: bfloat16 [16, 2048, 16], P('wt'), may hold values from -0.125 to 0.125
- adapter_up: bfloat16 [16, 16, 3, 2048], P(None, None, None, 'wt'), may hold values from -1.5 to 1.5
- out_weight: bfloat16 [2048, 2048], P('req', 'wt'), may hold values from -0.125 to 0.125
- page_slot: int32 [2048], P('req'), may hold values from 0 to 2047, as said below
Outputs:
- new_streams: bfloat16 [4, 32768, 2048], P(None, 'req', 'wt')
- kv_pool: bfloat16 [2048, 16, 2, 2048], P('req', None, None, 'wt')
Inputs may be any that keep to these rules, and one draw needn't show every extreme that they name: page_slot is a permutation of all page slots; page p lands on index page_slot[p] // 32 of req; the pages 2k and 2k + 1 form one request and land on the same index; of the pages of one index of req at most 2 land on any one index, and exactly 2 on some.
All inputs are finite; a program needn't handle non-finite values.
Results may differ from a plain program's by a relative error of at most 0.008.
Values may be sent and summed in bfloat16 or wider, within the bound.
A program may use at most 64 MiB of HBM per device.

v0:
```python
import math
import jax
import jax.numpy as jnp
from jax import lax
from jax.sharding import PartitionSpec as P

HD = 128
R = 16
PAGE = 16
EPSILON = 1e-05


def body(
    streams,
    doc_ids,
    doc_adapter,
    width_weights,
    stream_mixing,
    depth_static,
    depth_dir,
    qkv_weight,
    adapter_down,
    adapter_up,
    out_weight,
    page_slot,
):
    count_streams = streams.shape[0]
    tokens = streams.shape[1]
    mixed_local = width_weights[0] * streams[0].astype(jnp.float32)
    for stream in range(1, count_streams):
        mixed_local = mixed_local + width_weights[stream] * streams[stream].astype(jnp.float32)
    gathered = lax.all_gather(mixed_local.astype(jnp.bfloat16), "wt", axis=1, tiled=True)
    widened = gathered.astype(jnp.float32)
    normed = (
        widened * lax.rsqrt(jnp.mean(widened * widened, axis=-1, keepdims=True) + EPSILON)
    ).astype(jnp.bfloat16)
    segment = doc_ids[0]
    doc_table = doc_adapter[0, :, 0]
    token_adapter = jnp.sum(
        jnp.where(
            segment[:, None] == jnp.arange(doc_table.shape[0])[None, :], doc_table[None, :], 0
        ),
        axis=1,
    )
    adapters_total = adapter_up.shape[0]
    selector = (token_adapter[:, None] == jnp.arange(adapters_total)[None, :]).astype(jnp.float32)
    every_rank = jnp.einsum(
        "td,adr->tar",
        normed,
        lax.all_gather(adapter_down, "wt", axis=0, tiled=True),
        preferred_element_type=jnp.float32,
    )
    shrunk = jnp.sum(selector[:, :, None] * every_rank, axis=1)
    shrunk = shrunk.astype(jnp.bfloat16)
    spread = (
        (selector[:, :, None] * shrunk.astype(jnp.float32)[:, None, :])
        .reshape(tokens, adapters_total * R)
        .astype(jnp.bfloat16)
    )
    lowrank = jnp.dot(
        spread, adapter_up.reshape(adapters_total * R, -1), preferred_element_type=jnp.float32
    )
    width_local = qkv_weight.shape[2]
    portion = lax.all_gather(qkv_weight, "req", axis=0, tiled=True)
    base = jnp.dot(
        normed, portion.reshape(portion.shape[0], -1), preferred_element_type=jnp.float32
    )
    heads_local = width_local // HD
    projected = (base + lowrank).astype(jnp.bfloat16).reshape(tokens, 3, heads_local, HD)
    key_rows = projected[:, 1]
    value_rows = projected[:, 2]
    block_rows = min(512, tokens)
    blocks = tokens // block_rows
    positions = jnp.arange(tokens)

    def attend(packed):
        query_block, query_pos, query_seg = packed
        scores = jnp.einsum(
            "qhd,khd->hqk", query_block, key_rows, preferred_element_type=jnp.float32
        ) / math.sqrt(HD)
        allowed = (query_seg[:, None] == segment[None, :]) & (
            positions[None, :] <= query_pos[:, None]
        )
        scores = jnp.where(allowed[None], scores, -1e30)
        highest = jnp.max(scores, axis=-1, keepdims=True)
        weights = jnp.exp(scores - highest)
        weights = (weights / jnp.sum(weights, axis=-1, keepdims=True)).astype(jnp.bfloat16)
        return jnp.einsum(
            "hqk,khd->qhd", weights, value_rows, preferred_element_type=jnp.float32
        ).astype(jnp.bfloat16)

    attended = lax.map(
        attend,
        (
            projected[:, 0].reshape(blocks, block_rows, heads_local, HD),
            positions.reshape(blocks, block_rows),
            segment.reshape(blocks, block_rows),
        ),
    )
    attended = attended.reshape(tokens, width_local)
    every_row = lax.all_gather(out_weight, "req", axis=0, tiled=True)
    own_rows = lax.all_to_all(every_row, "wt", split_axis=0, concat_axis=1, tiled=True)
    layer_out = lax.psum_scatter(
        jnp.dot(attended, own_rows, preferred_element_type=jnp.float32).astype(jnp.bfloat16),
        "wt",
        scatter_dimension=1,
        tiled=True,
    ).astype(jnp.float32)
    depth = depth_static[None, :] + jnp.tanh(
        jnp.dot(normed, depth_dir, preferred_element_type=jnp.float32)
    )
    outputs = []
    for stream in range(count_streams):
        carried = stream_mixing[stream, 0] * streams[0].astype(jnp.float32)
        for source in range(1, count_streams):
            carried = carried + stream_mixing[stream, source] * streams[source].astype(jnp.float32)
        outputs.append((carried + depth[:, stream][:, None] * layer_out).astype(jnp.bfloat16))
    new_streams = jnp.stack(outputs)
    page_count = page_slot.shape[0]
    cache = projected[:, 1:3].reshape(page_count, PAGE, 2, width_local)
    groups = lax.axis_size("req")
    capacity = 2 * max(1, page_count // (2 * groups))
    target_dev = page_slot // page_count
    local_slot = page_slot % page_count
    ordinal = jnp.arange(page_count)
    earlier = (target_dev[None, :] == target_dev[:, None]) & (ordinal[None, :] < ordinal[:, None])
    placement = target_dev * capacity + jnp.sum(earlier.astype(jnp.int32), axis=1)
    outgoing = (
        jnp.zeros((groups * capacity, PAGE, 2, width_local), jnp.bfloat16).at[placement].set(cache)
    )
    labels = (
        jnp.full((groups * capacity,), -1.0, jnp.bfloat16)
        .at[placement]
        .set(local_slot.astype(jnp.bfloat16))
    )
    incoming, arrived = (
        lax.all_to_all(outgoing, "req", split_axis=0, concat_axis=0, tiled=True),
        lax.all_to_all(labels, "req", split_axis=0, concat_axis=0, tiled=True),
    )
    slot_index = arrived.astype(jnp.int32)
    slot_index = jnp.where(slot_index < 0, page_count, slot_index)
    kv_pool = (
        jnp.zeros((page_count + 1, PAGE, 2, width_local), jnp.bfloat16)
        .at[slot_index]
        .set(incoming)[:page_count]
    )
    return (new_streams, kv_pool)


def solution(mesh):
    in_specs = (
        P(None, "req", "wt"),
        P("req", None),
        P("req", None, None),
        P(),
        P(),
        P(),
        P(),
        P("req", None, "wt"),
        P("wt", None, None),
        P(None, None, None, "wt"),
        P("req", "wt"),
        P("req"),
    )
    out_specs = (P(None, "req", "wt"), P("req", None, None, "wt"))
    return jax.shard_map(body, mesh=mesh, in_specs=in_specs, out_specs=out_specs, check_vma=False)
```

profile of v0, /device:TPU:1, one launch (start us, length us, event | category | flops | bytes accessed | tf_op | source)
XLA Modules:
  0.0 408.4 jit_solution(16914693759775817778)
XLA Ops:
  7.2 0.7 all-gather.10.cloned.1.call-update
  8.0 1.5 fusion.59
  9.4 4.6 %fusion.24 = bf16[1,512,256]{2,1,0:T(8,128)(2,1)} fusion(f32[]{:T(128)} %bitcast.8, f32[]{:T(128)} %bitcast.7, f32[]{:T(128)} %bitcast.6, f32[]{:T(128)} %bitcast.5, bf16[4,512,256]{2,1,0:T(8,128)(2,1)} %param.12), kind=kLoop, calls=%fused_computation.62 | loop fusion | flops 1572864 | bytes 1310736 | tf_op jit(solution)/shard_map/convert_element_type | solution.py:32
  14.1 0.7 all-gather.8.cloned.1.call-update
  14.9 0.5 all-gather.6.cloned.1.call-update
  15.4 84.8 %all-gather.10.cloned.1.call-done = bf16[2048,256]{1,0:T(8,128)(2,1)} async-done(((bf16[32,256]{1,0:T(8,128)(2,1)}), bf16[2048,256]{1,0:T(8,128)(2,1)}) %all-gather.10.cloned.1.call-update) | async-done | bytes 1048592 | tf_op jit(solution)/shard_map/all_gather | solution.py:101
  100.2 6.5 %all-to-all-start = ((bf16[8,256,256]{2,1,0:T(8,128)(2,1)}), bf16[8,256,256]{2,1,0:T(8,128)(2,1)S(1)}, u32[]{:S(2)}, u32[]{:S(2)}) async-start(bf16[8,256,256]{2,1,0:T(8,128)(2,1)} %bitcast.120), calls=%async_computation | async-start | bytes 2097152 | tf_op jit(solution)/shard_map/all_to_all | solution.py:102
  106.7 0.5 fusion.45
  107.2 0.3 copy.50
  107.6 0.7 convert_reduce_fusion.1
  108.4 0.6 fusion.43
  109.0 0.9 fusion.7
  109.9 50.0 %all-gather.12.cloned.1.call-done = bf16[1,512,2048]{2,1,0:T(8,128)(2,1)} async-done(((bf16[1,512,256]{2,1,0:T(8,128)(2,1)}), bf16[1,512,2048]{2,1,0:T(8,128)(2,1)}) %all-gather.12.cloned.1.call-update) | async-done | bytes 2097168 | tf_op jit(solution)/shard_map/all_gather | solution.py:32
  159.9 2.2 fusion.1
  162.2 0.6 add_rsqrt_fusion
  162.8 34.9 %all-gather.8.cloned.1.call-done = bf16[16,2048,16]{1,2,0:T(8,128)(2,1)} async-done(((bf16[2,2048,16]{1,2,0:T(8,128)(2,1)}), bf16[16,2048,16]{1,2,0:T(8,128)(2,1)}) %all-gather.8.cloned.1.call-update) | async-done | bytes 1048592 | tf_op jit(solution)/shard_map/all_gather | solution.py:50
  197.7 2.1 fusion.51
  199.9 0.5 copy.55
  200.4 88.9 %all-gather.6.cloned.1.call-done = bf16[2048,3,256]{2,0,1:T(8,128)(2,1)} async-done(((bf16[32,3,256]{2,0,1:T(8,128)(2,1)}), bf16[2048,3,256]{2,0,1:T(8,128)(2,1)}) %all-gather.6.cloned.1.call-update) | async-done | bytes 3145744 | tf_op jit(solution)/shard_map/all_gather | solution.py:64
  289.4 4.7 %copy.49 = bf16[2048,3,256]{0,2,1:T(8,128)(2,1)} copy(bf16[2048,3,256]{2,0,1:T(8,128)(2,1)} %all-gather.6.cloned.1.call-done) | data formatting | bytes 6291456 | tf_op jit(solution)/shard_map/all_gather | solution.py:64
  294.1 4.4 %fusion.53 = f32[512,768]{1,0:T(8,128)S(1)} fusion(bf16[2048,768]{0,1:T(8,128)(2,1)} %bitcast.116, bf16[1,512,2048]{2,1,0:T(8,128)(2,1)} %all-gather.12.cloned.1.call-done, f32[512]{0:T(512)S(1)} %copy-done.9), kind=kOutput, calls=%fused_computation.110 | convolution fusion | flops 1613758464 | bytes 6817792 | tf_op jit(solution)/shard_map/dot_general | solution.py:65
  298.5 0.4 add_convert_fusion
  298.9 0.2 reshape.208
  299.1 0.5 fusion.56
  299.6 0.2 copy.61
  299.9 2.3 fusion.60
  302.1 1.9 convolution_convert_fusion.1
  304.1 2.1 convolution_convert_fusion
  306.2 0.9 scatter_custom_fusion
  307.1 0.8 all_to_all.30
  307.9 6.3 %all-to-all-start.1 = ((bf16[64,2,1]{1,2,0:T(2,128)(2,1)}), bf16[64,2,1]{1,2,0:T(2,128)(2,1)S(1)}, u32[]{:S(2)}, u32[]{:S(2)}) async-start(bf16[64,2,1]{1,2,0:T(2,128)(2,1)} %all_to_all.30), calls=%async_computation.2 | async-start | bytes 65536 | tf_op jit(solution)/shard_map/all_to_all | solution.py:138
  314.2 0.4 slice.155
  314.6 0.3 reshape.251
  314.9 0.1 copy.58
  315.0 1.6 broadcast_in_dim.85
  316.6 4.3 %scatter_fusion = bf16[128,16,2,256]{3,1,2,0:T(8,128)(2,1)} fusion(bf16[128,16,2,256]{3,1,2,0:T(8,128)(2,1)} %broadcast_in_dim.85, s32[32]{0:T(128)S(1)} %compare_select_fusion.2, bf16[32,16,2,256]{3,1,2,0:T(8,128)(2,1)S(1)} %copy.58), kind=kCustom, calls=%fused_computation.1 | custom fusion | bytes 1572992 | tf_op jit(solution)/shard_map/scatter | solution.py:129
  321.0 2.5 all-to-all-done.1
  323.5 8.1 %all-to-all-start.2 = ((bf16[128,16,2,256]{3,1,2,0:T(8,128)(2,1)}), bf16[128,16,2,256]{3,1,2,0:T(8,128)(2,1)S(1)}, u32[]{:S(2)}, u32[]{:S(2)}) async-start(bf16[128,16,2,256]{3,1,2,0:T(8,128)(2,1)} %scatter_fusion), calls=%async_computation.3 | async-start | bytes 4194304 | tf_op jit(solution)/shard_map/all_to_all | solution.py:137
  331.5 0.7 fusion.58
  332.3 0.1 convert_reduce_fusion
  332.4 0.1 reshape.216
  332.6 2.3 fusion.4
  334.9 47.8 %all-to-all-done.2 = bf16[128,16,2,256]{3,1,2,0:T(8,128)(2,1)S(1)} async-done(((bf16[128,16,2,256]{3,1,2,0:T(8,128)(2,1)}), bf16[128,16,2,256]{3,1,2,0:T(8,128)(2,1)S(1)}, u32[]{:S(2)}, u32[]{:S(2)}) %all-to-all-start.2) | async-done | bytes 2097184 | tf_op jit(solution)/shard_map/all_to_all | solution.py:137
  382.8 4.6 %scatter_fusion.1 = bf16[33,16,2,256]{3,1,2,0:T(8,128)(2,1)S(1)} fusion(bf16[33,16,2,256]{3,1,2,0:T(8,128)(2,1)S(1)} %broadcast_in_dim.81, s32[128]{0:T(128)S(1)} %fusion.46, bf16[128,16,2,256]{3,1,2,0:T(8,128)(2,1)S(1)} %all-to-all-done.2), kind=kCustom, calls=%fused_computation.2 | custom fusion | bytes 6291968 | tf_op jit(solution)/shard_map/scatter | solution.py:145
  387.5 1.3 copy.59
  388.8 6.4 %fusion.40 = (bf16[1,512,256]{2,1,0:T(8,128)(2,1)S(1)}, bf16[1,512,256]{2,1,0:T(8,128)(2,1)S(1)}) fusion(bf16[512,256]{1,0:T(8,128)(2,1)} %reduce-scatter.2.cloned.1.call-done, f32[512]{0:T(512)S(1)} %bitcast.128, f32[]{:T(128)} %bitcast.38, f32[]{:T(128)} %bitcast.37, f32[]{:T(128)} %bitcast.36, f32[]{:T(128)} %bitcast.35, ...), kind=kLoop, calls=%fused_computation.82 | loop fusion | flops 3276800 | bytes 1839136 | tf_op jit(solution)/shard_map/stack | solution.py:118
  395.3 5.5 %fusion.42 = (bf16[1,512,256]{2,1,0:T(8,128)(2,1)S(1)}, bf16[1,512,256]{2,1,0:T(8,128)(2,1)S(1)}) fusion(bf16[512,256]{1,0:T(8,128)(2,1)S(1)} %copy-done.3, f32[512]{0:T(512)S(1)} %bitcast.125, f32[]{:T(128)} %bitcast.3, f32[]{:T(128)} %bitcast.2, f32[]{:T(128)} %bitcast.1, f32[]{:T(128)} %bitcast, bf16[4,512,256]{2,1,0:T(8,128)(2,1)S(1)} %copy-done.1, ...), kind=kLoop, calls=%fused_computation.84 | loop fusion | flops 3276800 | bytes 1839136 | tf_op jit(solution)/shard_map/stack | solution.py:118
  400.7 1.1 pad_maximum_fusion
  (53 shorter events, 0.7 us)
Async XLA Ops:
  7.2 325.4 %copy-start = (bf16[2048,4]{0,1:T(4,128)(2,1)S(1)}, bf16[2048,4]{0,1:T(4,128)(2,1)}, u32[]{:S(2)}) copy-start(bf16[2048,4]{0,1:T(4,128)(2,1)} %param.18) | copy-start | bytes 49156
  7.2 99.5 %copy-start.12 = (s32[32]{0:T(128)S(1)}, s32[32]{0:T(128)}, u32[]{:S(2)}) copy-start(s32[32]{0:T(128)} %param.23) | copy-start | bytes 388
  7.2 100.0 %copy-start.4 = (bf16[16,16,3,256]{3,1,2,0:T(8,128)(2,1)S(1)}, bf16[16,16,3,256]{3,1,2,0:T(8,128)(2,1)}, u32[]{:S(2)}) copy-start(bf16[16,16,3,256]{3,1,2,0:T(8,128)(2,1)} %param.21) | copy-start | bytes 1179652
  7.2 93.0 %all-gather.10.cloned.1.call-start = ((), (), s32[]{:S(2)}) async-start(), calls=%async_computation.6 | async-start | bytes 1064960 | tf_op jit(solution)/shard_map/all_gather | solution.py:101
  7.9 152.0 %all-gather.12.cloned.1.call-start = ((), (), s32[]{:S(2)}) async-start(), calls=%async_computation.8 | async-start | bytes 2359296 | tf_op jit(solution)/shard_map/all_gather | solution.py:32
  14.1 94.2 %copy-start.8 = (s32[1,512]{1,0:T(1,128)S(1)}, s32[1,512]{1,0:T(1,128)}, u32[]{:S(2)}) copy-start(s32[1,512]{1,0:T(1,128)} %param.13) | copy-start | bytes 6148
  14.1 94.2 %copy-start.11 = (s32[1,4,1]{1,2,0:T(1,128)S(1)}, s32[1,4,1]{1,2,0:T(1,128)}, u32[]{:S(2)}) copy-start(s32[1,4,1]{1,2,0:T(1,128)} %param.14) | copy-start | bytes 52
  14.1 183.6 %all-gather.8.cloned.1.call-start = ((), (), s32[]{:S(2)}) async-start(), calls=%async_computation.5 | async-start | bytes 1179648 | tf_op jit(solution)/shard_map/all_gather | solution.py:50
  14.8 274.5 %all-gather.6.cloned.1.call-start = ((), (), s32[]{:S(2)}) async-start(), calls=%async_computation.4 | async-start | bytes 3194880 | tf_op jit(solution)/shard_map/all_gather | solution.py:64
  100.2 99.7 %all-to-all-start = ((bf16[8,256,256]{2,1,0:T(8,128)(2,1)}), bf16[8,256,256]{2,1,0:T(8,128)(2,1)S(1)}, u32[]{:S(2)}, u32[]{:S(2)}) async-start(bf16[8,256,256]{2,1,0:T(8,128)(2,1)} %bitcast.120), calls=%async_computation | async-start | bytes 2097152 | tf_op jit(solution)/shard_map/all_to_all | solution.py:102
  106.7 282.2 %reduce-scatter.2.cloned.1.call-start = ((), (), s32[]{:S(2)}) async-start(), calls=%async_computation.7 | async-start | bytes 2359296 | tf_op jit(solution)/shard_map/reduce_scatter | solution.py:103
  107.2 1.8 copy-start.14
  159.9 37.7 %copy-start.2 = (bf16[1,512,2048]{2,1,0:T(8,128)(2,1)S(1)}, bf16[1,512,2048]{2,1,0:T(8,128)(2,1)}, u32[]{:S(2)}) copy-start(bf16[1,512,2048]{2,1,0:T(8,128)(2,1)} %all-gather.12.cloned.1.call-done) | copy-start | bytes 6291460
  197.7 2.1 copy-start.5
  200.4 93.7 %copy-start.9 = (f32[512]{0:T(512)S(1)}, f32[512]{0:T(512)}, u32[]{:S(2)}) copy-start(f32[512]{0:T(512)} %add_rsqrt_fusion) | copy-start | bytes 6148
  298.9 1.0 copy-start.6
  304.0 2.1 copy-start.15
  304.1 2.1 copy-start.16
  307.9 15.6 %all-to-all-start.1 = ((bf16[64,2,1]{1,2,0:T(2,128)(2,1)}), bf16[64,2,1]{1,2,0:T(2,128)(2,1)S(1)}, u32[]{:S(2)}, u32[]{:S(2)}) async-start(bf16[64,2,1]{1,2,0:T(2,128)(2,1)} %all_to_all.30), calls=%async_computation.2 | async-start | bytes 65536 | tf_op jit(solution)/shard_map/all_to_all | solution.py:138
  321.0 10.6 %copy-start.7 = (f32[4,4]{1,0:T(4,128)S(1)}, f32[4,4]{1,0:T(4,128)}, u32[]{:S(2)}) copy-start(f32[4,4]{1,0:T(4,128)} %param.16) | copy-start | bytes 196
  321.0 11.5 %copy-start.10 = (f32[512]{0:T(512)S(1)}, f32[512]{0:T(512)}, u32[]{:S(2)}) copy-start(f32[512]{0:T(512)} %add_rsqrt_fusion) | copy-start | bytes 6148
  321.0 11.6 %copy-start.13 = (f32[4]{0:T(128)S(1)}, f32[4]{0:T(128)}, u32[]{:S(2)}) copy-start(f32[4]{0:T(128)} %param.17) | copy-start | bytes 52
  323.5 59.3 %all-to-all-start.2 = ((bf16[128,16,2,256]{3,1,2,0:T(8,128)(2,1)}), bf16[128,16,2,256]{3,1,2,0:T(8,128)(2,1)S(1)}, u32[]{:S(2)}, u32[]{:S(2)}) async-start(bf16[128,16,2,256]{3,1,2,0:T(8,128)(2,1)} %scatter_fusion), calls=%async_computation.3 | async-start | bytes 4194304 | tf_op jit(solution)/shard_map/all_to_all | solution.py:137
  387.4 1.4 copy-start.1
  388.8 6.4 %copy-start.3 = (bf16[512,256]{1,0:T(8,128)(2,1)S(1)}, bf16[512,256]{1,0:T(8,128)(2,1)}, u32[]{:S(2)}) copy-start(bf16[512,256]{1,0:T(8,128)(2,1)} %reduce-scatter.2.cloned.1.call-done) | copy-start | bytes 786436
Sparse Core Ops, SparseCore 0:
  11.4 88.7 all-gather.9
  102.8 57.1 all-gather.11
  162.0 35.5 all-gather.7
  200.9 88.4 all-gather.5
  306.3 37.3 reduce-scatter.1
where the time goes:
time: 409 us; the launch traced here: 408 us
  waiting for transfers between devices  311 us (76%)
  other arithmetic  23.5 us (6%)
  local copies, waits for them, and re-layouts  23.4 us (6%)
  starting transfers between devices  21 us (5%)
  matrix products  15.4 us (4%)
  between operations  14.1 us (3%)
    all_gather x1, waiting for transfers between devices, body(): portion = lax.all_gather(qkv_weight, 'req', axis=0, tiled=True)  88.9 us
    all_gather x1, waiting for transfers between devices, body(): every_row = lax.all_gather(out_weight, 'req', axis=0, tiled=True)  84.8 us
    all_gather x1, waiting for transfers between devices, body(): lax.all_gather(mixed_local.astype(jnp.bfloat16), 'wt', axis=1, tiled=True)  50 us
    all_to_all x1, waiting for transfers between devices, body(): lax.all_to_all(outgoing, 'req', split_axis=0, concat_axis=0, tiled=True)  47.8 us
    all_gather x1, waiting for transfers between devices, body(): lax.all_gather(adapter_down, 'wt', axis=0, tiled=True)  34.9 us
    another operation x3, other arithmetic, body(): new_streams = jnp.stack(outputs)  13 us
  transfers between devices with their start and end apart: 8, of which 6 were waited for; matrix products, arithmetic and copies ran while one was open for 8% of the time, Pallas kernels for 0%

commit v1 on v0

--- a/solution.py
+++ b/solution.py
@@ -8,6 +8,12 @@
 R = 16
 PAGE = 16
 EPSILON = 1e-05
+
+
+def gather_from_all(x, axis, dim):
+    size = lax.axis_size(axis)
+    repeats = [size if d == dim else 1 for d in range(x.ndim)]
+    return lax.all_to_all(jnp.tile(x, repeats), axis, split_axis=dim, concat_axis=dim, tiled=True)
 
 
 def body(
@@ -47,7 +53,7 @@
     every_rank = jnp.einsum(
         "td,adr->tar",
         normed,
-        lax.all_gather(adapter_down, "wt", axis=0, tiled=True),
+        gather_from_all(adapter_down, "wt", 0),
         preferred_element_type=jnp.float32,
     )
     shrunk = jnp.sum(selector[:, :, None] * every_rank, axis=1)

time: 409 us -> 367 us (0.90)
  waiting for transfers between devices: 311 us -> 237 us
  blocking collectives: 0 us -> 33.6 us
    all_gather x1 -> x0, waiting for transfers between devices: 34.9 us -> none  [body(): lax.all_gather(adapter_down, 'wt', axis=0, tiled=True)]
    all_gather x1, waiting for transfers between devices: 84.8 us -> 50.8 us  [body(): every_row = lax.all_gather(out_weight, 'req', axis=0, tiled=True)]
    all_to_all x0 -> x1, blocking collectives: none -> 33.6 us  [gather_from_all(): lax.all_to_all(jnp.tile(x, repeats), axis, split_axis=dim, concat_axis=di...]
    all_gather x1, waiting for transfers between devices: 88.9 us -> 83.9 us  [body(): portion = lax.all_gather(qkv_weight, 'req', axis=0, tiled=True)]
  transfers between devices with their start and end apart: 8 -> 7, of which waited for: 6 -> 5; matrix products, arithmetic and copies ran while one was open for 8% -> 8% of each run, Pallas kernels for 0% -> 0%
where the time goes in v1:
time: 367 us; the launch traced here: 366 us
  waiting for transfers between devices  237 us (65%)
  blocking collectives  33.6 us (9%)
  local copies, waits for them, and re-layouts  24.3 us (7%)
  other arithmetic  22.2 us (6%)
  starting transfers between devices  21 us (6%)
  matrix products  14.3 us (4%)
  between operations  14.1 us (4%)
    all_gather x1, waiting for transfers between devices, body(): portion = lax.all_gather(qkv_weight, 'req', axis=0, tiled=True)  83.9 us
    all_gather x1, waiting for transfers between devices, body(): every_row = lax.all_gather(out_weight, 'req', axis=0, tiled=True)  50.8 us
    all_gather x1, waiting for transfers between devices, body(): lax.all_gather(mixed_local.astype(jnp.bfloat16), 'wt', axis=1, tiled=True)  50.5 us
    all_to_all x1, waiting for transfers between devices, body(): lax.all_to_all(outgoing, 'req', split_axis=0, concat_axis=0, tiled=True)  47.8 us
    all_to_all x1, blocking collectives, gather_from_all(): lax.all_to_all(jnp.tile(x, repeats), axis, split_axis=dim, concat_axis=di...  33.6 us
    another operation x3, other arithmetic, body(): new_streams = jnp.stack(outputs)  12.9 us
    all_to_all x1, starting transfers between devices, body(): lax.all_to_all(outgoing, 'req', split_axis=0, concat_axis=0, tiled=True)  8.03 us
  transfers between devices with their start and end apart: 7, of which 5 were waited for; matrix products, arithmetic and copies ran while one was open for 8% of the time, Pallas kernels for 0%

profile of v1, /device:TPU:1, one launch (start us, length us, event | category | flops | bytes accessed | tf_op | source)
XLA Modules:
  0.0 366.5 jit_solution(3696277062531773913)
XLA Ops:
  7.2 0.7 all-gather.7.cloned.1.call-update
  8.0 1.4 fusion.59
  9.4 4.6 %fusion.24 = bf16[1,512,256]{2,1,0:T(8,128)(2,1)} fusion(f32[]{:T(128)} %bitcast.8, f32[]{:T(128)} %bitcast.7, f32[]{:T(128)} %bitcast.6, f32[]{:T(128)} %bitcast.5, bf16[4,512,256]{2,1,0:T(8,128)(2,1)} %param.12), kind=kLoop, calls=%fused_computation.62 | loop fusion | flops 1572864 | bytes 1310736 | tf_op jit(solution)/shard_map/convert_element_type | solution.py:38
  14.0 0.7 all-gather.5.cloned.1.call-update
  14.7 1.0 tile.4
  15.8 33.6 %all_to_all.39 = bf16[16,2048,16]{1,2,0:T(8,128)(2,1)S(1)} all-to-all(bf16[16,2048,16]{1,2,0:T(8,128)(2,1)S(1)} %bitcast.117), channel_id=1, replica_groups=mesh['req'=64,'wt'=8] {'wt'}, dimensions={0} | all-to-all | bytes 2097152 | tf_op jit(solution)/shard_map/all_to_all | solution.py:16
  49.4 50.8 %all-gather.7.cloned.1.call-done = bf16[2048,256]{1,0:T(8,128)(2,1)} async-done(((bf16[32,256]{1,0:T(8,128)(2,1)}), bf16[2048,256]{1,0:T(8,128)(2,1)}) %all-gather.7.cloned.1.call-update) | async-done | bytes 1048592 | tf_op jit(solution)/shard_map/all_gather | solution.py:107
  100.2 6.5 %all-to-all-start.1 = ((bf16[8,256,256]{2,1,0:T(8,128)(2,1)}), bf16[8,256,256]{2,1,0:T(8,128)(2,1)S(1)}, u32[]{:S(2)}, u32[]{:S(2)}) async-start(bf16[8,256,256]{2,1,0:T(8,128)(2,1)} %bitcast.122), calls=%async_computation.1 | async-start | bytes 2097152 | tf_op jit(solution)/shard_map/all_to_all | solution.py:108
  106.7 0.6 fusion.45
  107.3 0.3 copy.50
  107.7 0.8 convert_reduce_fusion.1
  108.4 0.1 select_reduce_fusion
  108.5 0.9 fusion.7
  109.4 50.5 %all-gather.9.cloned.1.call-done = bf16[1,512,2048]{2,1,0:T(8,128)(2,1)} async-done(((bf16[1,512,256]{2,1,0:T(8,128)(2,1)}), bf16[1,512,2048]{2,1,0:T(8,128)(2,1)}) %all-gather.9.cloned.1.call-update) | async-done | bytes 2097168 | tf_op jit(solution)/shard_map/all_gather | solution.py:38
  159.9 2.2 fusion.1
  162.2 0.9 fusion.51
  163.1 0.1 multiply_reduce_fusion
  163.2 0.5 copy.55
  163.8 83.9 %all-gather.5.cloned.1.call-done = bf16[2048,3,256]{2,0,1:T(8,128)(2,1)} async-done(((bf16[32,3,256]{2,0,1:T(8,128)(2,1)}), bf16[2048,3,256]{2,0,1:T(8,128)(2,1)}) %all-gather.5.cloned.1.call-update) | async-done | bytes 3145744 | tf_op jit(solution)/shard_map/all_gather | solution.py:70
  247.7 4.7 %copy.49 = bf16[2048,3,256]{0,2,1:T(8,128)(2,1)} copy(bf16[2048,3,256]{2,0,1:T(8,128)(2,1)} %all-gather.5.cloned.1.call-done) | data formatting | bytes 6291456 | tf_op jit(solution)/shard_map/all_gather | solution.py:70
  252.4 4.4 %fusion.53 = f32[512,768]{1,0:T(8,128)S(1)} fusion(bf16[2048,768]{0,1:T(8,128)(2,1)} %bitcast.118, bf16[1,512,2048]{2,1,0:T(8,128)(2,1)} %all-gather.9.cloned.1.call-done, f32[512]{0:T(512)S(1)} %add_rsqrt_fusion), kind=kOutput, calls=%fused_computation.110 | convolution fusion | flops 1613758464 | bytes 6817792 | tf_op jit(solution)/shard_map/dot_general | solution.py:71
  256.7 0.4 add_convert_fusion
  257.2 0.2 reshape.212
  257.3 0.5 fusion.56
  257.9 0.2 copy.61
  258.1 2.3 fusion.60
  260.4 1.9 convolution_convert_fusion.1
  262.3 2.1 convolution_convert_fusion
  264.5 0.9 scatter_custom_fusion
  265.4 0.8 all_to_all.34
  266.2 6.3 %all-to-all-start.2 = ((bf16[64,2,1]{1,2,0:T(2,128)(2,1)}), bf16[64,2,1]{1,2,0:T(2,128)(2,1)S(1)}, u32[]{:S(2)}, u32[]{:S(2)}) async-start(bf16[64,2,1]{1,2,0:T(2,128)(2,1)} %all_to_all.34), calls=%async_computation.3 | async-start | bytes 65536 | tf_op jit(solution)/shard_map/all_to_all | solution.py:144
  272.5 0.4 slice.155
  272.9 0.3 reshape.255
  273.2 0.1 copy.58
  273.3 1.6 broadcast_in_dim.85
  274.9 4.4 %scatter_fusion = bf16[128,16,2,256]{3,1,2,0:T(8,128)(2,1)} fusion(bf16[128,16,2,256]{3,1,2,0:T(8,128)(2,1)} %broadcast_in_dim.85, s32[32]{0:T(128)S(1)} %compare_select_fusion.2, bf16[32,16,2,256]{3,1,2,0:T(8,128)(2,1)S(1)} %copy.58), kind=kCustom, calls=%fused_computation.1 | custom fusion | bytes 1572992 | tf_op jit(solution)/shard_map/scatter | solution.py:135
  279.2 2.5 all-to-all-done.2
  281.7 8.0 %all-to-all-start.3 = ((bf16[128,16,2,256]{3,1,2,0:T(8,128)(2,1)}), bf16[128,16,2,256]{3,1,2,0:T(8,128)(2,1)S(1)}, u32[]{:S(2)}, u32[]{:S(2)}) async-start(bf16[128,16,2,256]{3,1,2,0:T(8,128)(2,1)} %scatter_fusion), calls=%async_computation.4 | async-start | bytes 4194304 | tf_op jit(solution)/shard_map/all_to_all | solution.py:143
  289.8 0.7 fusion.58
  290.5 0.1 convert_reduce_fusion
  290.6 0.1 reshape.220
  290.8 2.3 fusion.4
  293.1 47.8 %all-to-all-done.3 = bf16[128,16,2,256]{3,1,2,0:T(8,128)(2,1)S(1)} async-done(((bf16[128,16,2,256]{3,1,2,0:T(8,128)(2,1)}), bf16[128,16,2,256]{3,1,2,0:T(8,128)(2,1)S(1)}, u32[]{:S(2)}, u32[]{:S(2)}) %all-to-all-start.3) | async-done | bytes 2097184 | tf_op jit(solution)/shard_map/all_to_all | solution.py:143
  341.0 4.6 %scatter_fusion.1 = bf16[33,16,2,256]{3,1,2,0:T(8,128)(2,1)S(1)} fusion(bf16[33,16,2,256]{3,1,2,0:T(8,128)(2,1)S(1)} %broadcast_in_dim.81, s32[128]{0:T(128)S(1)} %fusion.46, bf16[128,16,2,256]{3,1,2,0:T(8,128)(2,1)S(1)} %all-to-all-done.3), kind=kCustom, calls=%fused_computation.2 | custom fusion | bytes 6291968 | tf_op jit(solution)/shard_map/scatter | solution.py:151
  345.7 1.3 copy.59
  347.0 6.4 %fusion.40 = (bf16[1,512,256]{2,1,0:T(8,128)(2,1)S(1)}, bf16[1,512,256]{2,1,0:T(8,128)(2,1)S(1)}) fusion(bf16[512,256]{1,0:T(8,128)(2,1)} %reduce-scatter.2.cloned.1.call-done, f32[512]{0:T(512)S(1)} %bitcast.131, f32[]{:T(128)} %bitcast.39, f32[]{:T(128)} %bitcast.38, f32[]{:T(128)} %bitcast.37, f32[]{:T(128)} %bitcast.36, ...), kind=kLoop, calls=%fused_computation.82 | loop fusion | flops 3276800 | bytes 1839136 | tf_op jit(solution)/shard_map/stack | solution.py:124
  353.5 5.3 %fusion.42 = (bf16[1,512,256]{2,1,0:T(8,128)(2,1)S(1)}, bf16[1,512,256]{2,1,0:T(8,128)(2,1)S(1)}) fusion(bf16[512,256]{1,0:T(8,128)(2,1)S(1)} %copy-done.3, f32[512]{0:T(512)S(1)} %bitcast.128, f32[]{:T(128)} %bitcast.3, f32[]{:T(128)} %bitcast.2, f32[]{:T(128)} %bitcast.1, f32[]{:T(128)} %bitcast, bf16[4,512,256]{2,1,0:T(8,128)(2,1)S(1)} %copy-done.1, ...), kind=kLoop, calls=%fused_computation.84 | loop fusion | flops 3276800 | bytes 1839136 | tf_op jit(solution)/shard_map/stack | solution.py:124
  358.8 1.1 pad_maximum_fusion
  (50 shorter events, 0.6 us)
Async XLA Ops:
  7.2 283.6 %copy-start = (bf16[2048,4]{0,1:T(4,128)(2,1)S(1)}, bf16[2048,4]{0,1:T(4,128)(2,1)}, u32[]{:S(2)}) copy-start(bf16[2048,4]{0,1:T(4,128)(2,1)} %param.18) | copy-start | bytes 49156
  7.2 93.0 %all-gather.7.cloned.1.call-start = ((), (), s32[]{:S(2)}) async-start(), calls=%async_computation.6 | async-start | bytes 1064960 | tf_op jit(solution)/shard_map/all_gather | solution.py:107
  7.9 152.0 %all-gather.9.cloned.1.call-start = ((), (), s32[]{:S(2)}) async-start(), calls=%async_computation.8 | async-start | bytes 2359296 | tf_op jit(solution)/shard_map/all_gather | solution.py:38
  14.0 233.7 %all-gather.5.cloned.1.call-start = ((), (), s32[]{:S(2)}) async-start(), calls=%async_computation.5 | async-start | bytes 3194880 | tf_op jit(solution)/shard_map/all_gather | solution.py:70
  15.7 91.0 %copy-start.11 = (s32[32]{0:T(128)S(1)}, s32[32]{0:T(128)}, u32[]{:S(2)}) copy-start(s32[32]{0:T(128)} %param.23) | copy-start | bytes 388
  15.7 91.6 %copy-start.4 = (bf16[16,16,3,256]{3,1,2,0:T(8,128)(2,1)S(1)}, bf16[16,16,3,256]{3,1,2,0:T(8,128)(2,1)}, u32[]{:S(2)}) copy-start(bf16[16,16,3,256]{3,1,2,0:T(8,128)(2,1)} %param.21) | copy-start | bytes 1179652
  49.4 59.0 %copy-start.7 = (s32[1,512]{1,0:T(1,128)S(1)}, s32[1,512]{1,0:T(1,128)}, u32[]{:S(2)}) copy-start(s32[1,512]{1,0:T(1,128)} %param.13) | copy-start | bytes 6148
  49.4 59.0 %copy-start.10 = (s32[1,4,1]{1,2,0:T(1,128)S(1)}, s32[1,4,1]{1,2,0:T(1,128)}, u32[]{:S(2)}) copy-start(s32[1,4,1]{1,2,0:T(1,128)} %param.14) | copy-start | bytes 52
  100.2 63.1 %all-to-all-start.1 = ((bf16[8,256,256]{2,1,0:T(8,128)(2,1)}), bf16[8,256,256]{2,1,0:T(8,128)(2,1)S(1)}, u32[]{:S(2)}, u32[]{:S(2)}) async-start(bf16[8,256,256]{2,1,0:T(8,128)(2,1)} %bitcast.122), calls=%async_computation.1 | async-start | bytes 2097152 | tf_op jit(solution)/shard_map/all_to_all | solution.py:108
  106.6 240.4 %reduce-scatter.2.cloned.1.call-start = ((), (), s32[]{:S(2)}) async-start(), calls=%async_computation.7 | async-start | bytes 2359296 | tf_op jit(solution)/shard_map/reduce_scatter | solution.py:109
  107.3 1.2 copy-start.13
  159.9 2.2 copy-start.2
  162.2 90.2 %copy-start.8 = (f32[512]{0:T(512)}, f32[512]{0:T(512)S(1)}, u32[]{:S(2)}) copy-start(f32[512]{0:T(512)S(1)} %add_rsqrt_fusion) | copy-start | bytes 6148
  257.2 1.0 copy-start.5
  262.3 2.1 copy-start.14
  262.3 2.1 copy-start.15
  266.2 15.6 %all-to-all-start.2 = ((bf16[64,2,1]{1,2,0:T(2,128)(2,1)}), bf16[64,2,1]{1,2,0:T(2,128)(2,1)S(1)}, u32[]{:S(2)}, u32[]{:S(2)}) async-start(bf16[64,2,1]{1,2,0:T(2,128)(2,1)} %all_to_all.34), calls=%async_computation.3 | async-start | bytes 65536 | tf_op jit(solution)/shard_map/all_to_all | solution.py:144
  279.2 10.5 %copy-start.6 = (f32[4,4]{1,0:T(4,128)S(1)}, f32[4,4]{1,0:T(4,128)}, u32[]{:S(2)}) copy-start(f32[4,4]{1,0:T(4,128)} %param.16) | copy-start | bytes 196
  279.2 11.5 %copy-start.9 = (f32[512]{0:T(512)S(1)}, f32[512]{0:T(512)}, u32[]{:S(2)}) copy-start(f32[512]{0:T(512)} %copy-done.8) | copy-start | bytes 6148
  279.2 11.5 %copy-start.12 = (f32[4]{0:T(128)S(1)}, f32[4]{0:T(128)}, u32[]{:S(2)}) copy-start(f32[4]{0:T(128)} %param.17) | copy-start | bytes 52
  281.7 59.2 %all-to-all-start.3 = ((bf16[128,16,2,256]{3,1,2,0:T(8,128)(2,1)}), bf16[128,16,2,256]{3,1,2,0:T(8,128)(2,1)S(1)}, u32[]{:S(2)}, u32[]{:S(2)}) async-start(bf16[128,16,2,256]{3,1,2,0:T(8,128)(2,1)} %scatter_fusion), calls=%async_computation.4 | async-start | bytes 4194304 | tf_op jit(solution)/shard_map/all_to_all | solution.py:143
  345.7 1.4 copy-start.1
  347.0 6.4 %copy-start.3 = (bf16[512,256]{1,0:T(8,128)(2,1)S(1)}, bf16[512,256]{1,0:T(8,128)(2,1)}, u32[]{:S(2)}) copy-start(bf16[512,256]{1,0:T(8,128)(2,1)} %reduce-scatter.2.cloned.1.call-done) | copy-start | bytes 786436
Sparse Core Ops, SparseCore 0:
  11.3 88.7 all-gather.6
  102.8 57.1 all-gather.8
  163.3 84.2 all-gather.4
  264.6 37.4 reduce-scatter.1
